TPU v7x, 256 devices: a whole 4x4x8 slice. The times are simulated.
256 devices in a mesh: row: 32 (over y, x, core), col: 8 (over z).
Axes of the slice: x: 4, y: 4, z: 8, core: 2. Of those that a mesh axis runs over, the one named last changes fastest.
Arguments:
- panel: float32 [24576, 256], P('row', 'col'), may hold values from -6 to 6
- trailing: float32 [24576, 12032], P('row', 'col'), may hold values from -6 to 6
Outputs:
- projections: float32 [12032, 256], P('col')
- remainder: float32 [24576, 12032], P('row', 'col')
All inputs are finite; a program needn't handle non-finite values.
Results may differ from a plain program's by a relative error of at most 0.000075.
Values sent between devices are 32-bit elements; how exact they have to be, the bound alone decides.
A program may use at most 64 MiB of HBM per device.

v0:
```python
import jax
import jax.numpy as jnp
from jax import lax
from jax.sharding import PartitionSpec as P


def cross_rows(left, right):
    return lax.dot_general(
        left,
        right,
        (((0,), (0,)), ((), ())),
        precision=lax.Precision.HIGHEST,
        preferred_element_type=jnp.float32,
    )


def solve_right(lower_factor, terms):
    return jax.scipy.linalg.solve_triangular(lower_factor, terms.T, lower=True).T


def per_device(panel, trailing):
    panel_full = lax.all_gather(panel, "col", axis=1, tiled=True)
    panel_gram = lax.psum(cross_rows(panel_full, panel_full), "row")
    lower_factor = jnp.linalg.cholesky(panel_gram)
    orthonormal = solve_right(lower_factor, panel_full)
    cross_terms = lax.psum(cross_rows(trailing, panel_full), "row")
    projections = solve_right(lower_factor, cross_terms)
    update = lax.dot_general(
        orthonormal,
        projections,
        (((1,), (1,)), ((), ())),
        precision=lax.Precision.HIGHEST,
        preferred_element_type=jnp.float32,
    )
    remainder = trailing - update
    return (projections, remainder)


def solution(mesh):
    return jax.shard_map(
        per_device,
        mesh=mesh,
        in_specs=(P("row", "col"), P("row", "col")),
        out_specs=(P("col", None), P("row", "col")),
        check_vma=False,
    )
```

profile of v0, /device:TPU:6, one launch (start us, length us, event | category | flops | bytes accessed | tf_op | source)
XLA Modules:
  0.0 242.3 jit_solution(3756788934562251100)
XLA Ops:
  7.2 30.0 %all_gather.3 = f32[768,256]{0,1:T(8,128)S(1)} all-gather(f32[768,32]{0,1:T(8,128)} %param.2), channel_id=1, replica_groups=mesh['row'=32,'col'=8] {'col'}, dimensions={1}, use_global_device_ids=true | all-gather | bytes 884736 | tf_op jit(solution)/shard_map/all_gather | solution.py:22
  37.2 1.5 fusion.18
  38.8 7.3 %fusion.19 = f32[256,1504]{0,1:T(8,128)} fusion(f32[768,256]{0,1:T(8,128)S(1)} %all_gather.3, f32[768,1504]{0,1:T(8,128)} %param.3), kind=kOutput, calls=%fused_computation.41 | convolution fusion | flops 3548381184 | bytes 6946816 | tf_op jit(solution)/shard_map/dot_general | solution.py:8
  46.1 116.7 %all-reduce.4.cloned.1.call-done = (f32[256,1504]{0,1:T(8,128)}, f32[256,256]{0,1:T(8,128)}) async-done(((f32[256,1504]{0,1:T(8,128)}, f32[256,256]{0,1:T(8,128)}), (f32[256,1504]{0,1:T(8,128)}, f32[256,256]{0,1:T(8,128)})) %all-reduce.4.cloned.1.call-update) | async-done | bytes 1802256 | tf_op jit(solution)/shard_map/psum | solution.py:26
  162.8 1.1 copy.5
  163.9 1.0 fusion.8
  165.0 11.7 %cholesky.50 = f32[128,128]{1,0:T(8,128)S(1)} custom-call(f32[128,128]{1,0:T(8,128)S(1)} %cholesky.118), custom_call_target="Cholesky" | custom-call | tf_op jit(solution)/shard_map/jit(cholesky)/cholesky | solution.py:24
  176.7 9.8 %custom-call.18 = f32[1,128,128]{1,2,0:T(8,128)S(1)} custom-call(f32[1,128,128]{2,1,0:T(8,128)S(1)} %get-tuple-element.25), custom_call_target="InvertDiagBlocksLowerTriangular" | custom-call | tf_op jit(solution)/shard_map/jit(cholesky)/cholesky | solution.py:24
  187.0 11.9 %cholesky.105 = f32[128,128]{1,0:T(8,128)S(1)} custom-call(f32[128,128]{1,0:T(8,128)S(1)} %convolution_subtract_fusion.3), custom_call_target="Cholesky" | custom-call | tf_op jit(solution)/shard_map/jit(cholesky)/cholesky | solution.py:24
  199.0 0.6 compare_reduce_fusion
  201.0 4.0 %while.1 = (s32[]{:T(128)}, f32[256,256]{1,0:T(8,128)S(1)}, s32[2,2]{1,0:T(2,128)S(1)}, f32[2,128,128]{2,1,0:T(8,128)S(1)}, s32[]{:T(128)}) while((s32[]{:T(128)}, f32[256,256]{1,0:T(8,128)S(1)}, s32[2,2]{1,0:T(2,128)S(1)}, f32[2,128,128]{2,1,0:T(8,128)S(1)}, s32[]{:T(128)}) %tuple.27), condition=%wide.while_cond, body=%wide.while_body.sunk | while | flops 2 | bytes 131181 | solution.py:18
  201.0 0.6 fusion.31
  201.6 1.4 bitcast_dynamic-update-slice_fusion.2
  203.0 0.6 fusion.31
  203.6 1.4 bitcast_dynamic-update-slice_fusion.2
  205.0 19.7 %custom-call.19 = f32[2,128,128]{1,2,0:T(8,128)S(1)} custom-call(f32[2,128,128]{2,1,0:T(8,128)S(1)} %get-tuple-element.9), custom_call_target="InvertDiagBlocksLowerTriangular" | custom-call | tf_op jit(solution)/shard_map/jit(_solve_triangular)/triangular_solve | solution.py:18
  224.7 0.5 fusion.6
  225.2 0.5 convolution_subtract_fusion.2
  225.7 0.5 fusion.12
  226.2 0.8 fusion.4
  227.0 0.8 convolution_subtract_fusion.1
  227.8 0.8 fusion.13
  228.6 1.2 fusion
  229.8 5.6 %convolution_subtract_fusion = f32[768,1504]{0,1:T(8,128)} fusion(f32[768,1504]{0,1:T(8,128)S(1)} %bitcast.45, f32[128,1504]{0,1:T(8,128)S(1)} %fusion.13, f32[128,1504]{0,1:T(8,128)S(1)} %fusion.4, f32[128,768]{1,0:T(8,128)S(1)} %fusion.12, f32[128,768]{1,0:T(8,128)S(1)} %fusion.6), kind=kOutput, calls=%fused_computation.2 | convolution fusion | flops 3550117888 | bytes 11567104 | tf_op jit(solution)/shard_map/dot_general | solution.py:28
  (21 shorter events, 0.8 us)
Async XLA Ops:
  7.2 155.7 %all-reduce.4.cloned.1.call-start = ((), (), s32[]{:S(2)}) async-start(), calls=%async_computation | async-start | bytes 3604480 | tf_op jit(solution)/shard_map/psum | solution.py:26
  163.9 65.9 %slice-start = ((s8[4620288]{0:T(1024)(128)(4,1)}), s8[425984]{0:T(1024)(128)(4,1)S(1)}, s32[]{:S(2)}) async-start(s8[4620288]{0:T(1024)(128)(4,1)} %bitcast.44), calls=%async_computation.1 | async-start | bytes 851968
  205.0 21.2 %copy-start = (f32[256,1504]{0,1:T(8,128)S(1)}, f32[256,1504]{0,1:T(8,128)}, u32[]{:S(2)}) copy-start(f32[256,1504]{0,1:T(8,128)} %get-tuple-element.18) | copy-start | bytes 4620292
  226.2 3.6 %slice-start.1 = ((s8[4620288]{0:T(1024)(128)(4,1)}), s8[4194304]{0:T(1024)(128)(4,1)S(1)}, s32[]{:S(2)}) async-start(s8[4620288]{0:T(1024)(128)(4,1)} %bitcast.44), calls=%async_computation.2 | async-start | bytes 8388608
Sparse Core Ops, SparseCore 0:
  46.2 116.5 all-reduce.3
where the time goes:
time: 243 us; the launch traced here: 242 us
  waiting for transfers between devices  117 us (48%)
  other arithmetic  56.1 us (23%)
  blocking collectives  30 us (12%)
  matrix products  18.8 us (8%)
  between operations  15.5 us (6%)
  local copies, waits for them, and re-layouts  5.15 us (2%)
    psum x1, waiting for transfers between devices, per_device(): cross_terms = lax.psum(cross_rows(trailing, panel_full), 'row')  117 us
    another operation x6, other arithmetic, per_device(): lower_factor = jnp.linalg.cholesky(panel_gram)  34.1 us
    all_gather x1, blocking collectives, per_device(): panel_full = lax.all_gather(panel, 'col', axis=1, tiled=True)  30 us
    another operation x3, other arithmetic, solve_right(): jax.scipy.linalg.solve_triangular(lower_factor, terms.T, lower=True)  19.7 us
    dot_general x2, matrix products, cross_rows(): lax.dot_general(left, right, (((0,), (0,)), ((), ())), precision=lax.Prec...  8.83 us
    dot_general x1, matrix products, per_device(): lax.dot_general(orthonormal, projections, (((1,), (1,)), ((), ())), preci...  5.64 us
  transfers between devices with their start and end apart: 1, of which 1 were waited for; matrix products, arithmetic and copies ran while one was open for 0% of the time, Pallas kernels for 0%

commit v1 on v0

--- a/solution.py
+++ b/solution.py
@@ -23,7 +23,7 @@
     panel_gram = lax.psum(cross_rows(panel_full, panel_full), "row")
     lower_factor = jnp.linalg.cholesky(panel_gram)
     orthonormal = solve_right(lower_factor, panel_full)
-    cross_terms = lax.psum(cross_rows(trailing, panel_full), "row")
+    cross_terms = jnp.sum(lax.all_gather(cross_rows(trailing, panel_full), "row"), axis=0)
     projections = solve_right(lower_factor, cross_terms)
     update = lax.dot_general(
         orthonormal,

time: 243 us -> 351 us (1.44)
  waiting for transfers between devices: 117 us -> 204 us
  other arithmetic: 56.1 us -> 74 us
    all_gather x0 -> x1, waiting for transfers between devices: none -> 99 us  [per_device(): lax.all_gather(cross_rows(trailing, panel_full), 'row')]
    reduce_sum x0 -> x1, other arithmetic: none -> 17.9 us  [per_device(): jnp.sum(lax.all_gather(cross_rows(trailing, panel_full), 'row'), axis=0)]
    psum x1, waiting for transfers between devices: 117 us -> 105 us  [per_device(): panel_gram = lax.psum(cross_rows(panel_full, panel_full), 'row')]
  transfers between devices with their start and end apart: 1 -> 2, of which waited for: 1 -> 2; matrix products, arithmetic and copies ran while one was open for 0% -> 20% of each run, Pallas kernels for 0% -> 0%
where the time goes in v1:
time: 351 us; the launch traced here: 349 us
  waiting for transfers between devices  204 us (58%)
  other arithmetic  74 us (21%)
  blocking collectives  30 us (9%)
  matrix products  20.4 us (6%)
  between operations  15.4 us (4%)
  local copies, waits for them, and re-layouts  4.93 us (1%)
    psum x1, waiting for transfers between devices, per_device(): panel_gram = lax.psum(cross_rows(panel_full, panel_full), 'row')  105 us
    all_gather x1, waiting for transfers between devices, per_device(): lax.all_gather(cross_rows(trailing, panel_full), 'row')  99 us
    another operation x6, other arithmetic, per_device(): lower_factor = jnp.linalg.cholesky(panel_gram)  34.1 us
    all_gather x1, blocking collectives, per_device(): panel_full = lax.all_gather(panel, 'col', axis=1, tiled=True)  30 us
    another operation x3, other arithmetic, solve_right(): jax.scipy.linalg.solve_triangular(lower_factor, terms.T, lower=True)  19.7 us
    reduce_sum x1, other arithmetic, per_device(): jnp.sum(lax.all_gather(cross_rows(trailing, panel_full), 'row'), axis=0)  17.9 us
    dot_general x2, matrix products, cross_rows(): lax.dot_general(left, right, (((0,), (0,)), ((), ())), precision=lax.Prec...  8.79 us
    dot_general x1, matrix products, per_device(): lax.dot_general(orthonormal, projections, (((1,), (1,)), ((), ())), preci...  7.3 us
  transfers between devices with their start and end apart: 2, of which 2 were waited for; matrix products, arithmetic and copies ran while one was open for 20% of the time, Pallas kernels for 0%

profile of v1, /device:TPU:6, one launch (start us, length us, event | category | flops | bytes accessed | tf_op | source)
XLA Modules:
  0.0 349.1 jit_solution(424194414774949908)
XLA Ops:
  7.2 30.0 %all_gather.9 = f32[768,256]{0,1:T(8,128)S(1)} all-gather(f32[768,32]{0,1:T(8,128)} %param.2), channel_id=1, replica_groups=mesh['row'=32,'col'=8] {'col'}, dimensions={1}, use_global_device_ids=true | all-gather | bytes 884736 | tf_op jit(solution)/shard_map/all_gather | solution.py:22
  37.2 1.5 fusion.18
  38.8 7.3 %fusion.19 = f32[1504,256]{1,0:T(8,128)} fusion(f32[768,1504]{0,1:T(8,128)} %param.3, f32[768,256]{0,1:T(8,128)S(1)} %all_gather.9), kind=kOutput, calls=%fused_computation.41 | convolution fusion | flops 3548381184 | bytes 6946816 | tf_op jit(solution)/shard_map/dot_general | solution.py:8
  46.1 105.2 %all-reduce.3.cloned.1.call-done = f32[256,256]{0,1:T(8,128)} async-done(((f32[256,256]{0,1:T(8,128)}), f32[256,256]{0,1:T(8,128)}) %all-reduce.3.cloned.1.call-update) | async-done | bytes 262160 | tf_op jit(solution)/shard_map/psum | solution.py:23
  151.3 1.1 copy.5
  152.4 1.0 fusion.8
  153.4 11.7 %cholesky.50 = f32[128,128]{1,0:T(8,128)S(1)} custom-call(f32[128,128]{1,0:T(8,128)S(1)} %cholesky.118), custom_call_target="Cholesky" | custom-call | tf_op jit(solution)/shard_map/jit(cholesky)/cholesky | solution.py:24
  165.2 9.8 %custom-call.18 = f32[1,128,128]{1,2,0:T(8,128)S(1)} custom-call(f32[1,128,128]{2,1,0:T(8,128)S(1)} %get-tuple-element.23), custom_call_target="InvertDiagBlocksLowerTriangular" | custom-call | tf_op jit(solution)/shard_map/jit(cholesky)/cholesky | solution.py:24
  175.5 11.9 %cholesky.105 = f32[128,128]{1,0:T(8,128)S(1)} custom-call(f32[128,128]{1,0:T(8,128)S(1)} %convolution_subtract_fusion.3), custom_call_target="Cholesky" | custom-call | tf_op jit(solution)/shard_map/jit(cholesky)/cholesky | solution.py:24
  187.4 0.6 compare_reduce_fusion
  189.4 3.8 %while.1 = (s32[]{:T(128)}, f32[256,256]{1,0:T(8,128)S(1)}, s32[2,2]{1,0:T(2,128)S(1)}, f32[2,128,128]{2,1,0:T(8,128)S(1)}, s32[]{:T(128)}) while((s32[]{:T(128)}, f32[256,256]{1,0:T(8,128)S(1)}, s32[2,2]{1,0:T(2,128)S(1)}, f32[2,128,128]{2,1,0:T(8,128)S(1)}, s32[]{:T(128)}) %tuple.27), condition=%wide.while_cond, body=%wide.while_body.sunk | while | flops 2 | bytes 131189 | solution.py:18
  189.4 0.6 fusion.31
  189.9 1.3 bitcast_dynamic-update-slice_fusion.2
  191.3 0.6 fusion.31
  191.9 1.3 bitcast_dynamic-update-slice_fusion.2
  193.1 19.7 %custom-call.19 = f32[2,128,128]{1,2,0:T(8,128)S(1)} custom-call(f32[2,128,128]{2,1,0:T(8,128)S(1)} %get-tuple-element.9), custom_call_target="InvertDiagBlocksLowerTriangular" | custom-call | tf_op jit(solution)/shard_map/jit(_solve_triangular)/triangular_solve | solution.py:18
  212.8 0.5 fusion.6
  214.4 99.0 %all-gather.3.cloned.1.call-done = f32[48128,256]{1,0:T(8,128)} async-done(((f32[1504,256]{1,0:T(8,128)}), f32[48128,256]{1,0:T(8,128)}) %all-gather.3.cloned.1.call-update) | async-done | bytes 49283088 | tf_op jit(solution)/shard_map/all_gather | solution.py:26
  313.4 17.9 %reduce_sum.9 = f32[1504,256]{1,0:T(8,128)S(1)} reduce(f32[32,1504,256]{2,1,0:T(8,128)} %bitcast.44, f32[]{:T(128)} %constant.85.clone.1), dimensions={0}, to_apply=%region_5.6 | reduce | flops 11935744 | bytes 50823172 | tf_op jit(solution)/shard_map/reduce_sum | solution.py:26
  331.3 0.8 fusion.4
  332.1 0.8 convolution_subtract_fusion.1
  332.9 0.8 fusion.13
  333.7 1.2 fusion
  334.9 7.3 %convolution_subtract_fusion = f32[768,1504]{0,1:T(8,128)} fusion(f32[768,1504]{0,1:T(8,128)} %param.3, f32[128,1504]{0,1:T(8,128)S(1)} %fusion.13, f32[128,1504]{0,1:T(8,128)S(1)} %fusion.4, f32[128,768]{1,0:T(8,128)S(1)} %fusion.12, f32[128,768]{1,0:T(8,128)S(1)} %fusion.6), kind=kOutput, calls=%fused_computation.2 | convolution fusion | flops 3550117888 | bytes 11567104 | tf_op jit(solution)/shard_map/dot_general | solution.py:28
  (18 shorter events, 1.8 us)
Async XLA Ops:
  7.2 144.2 %all-reduce.3.cloned.1.call-start = ((), (), s32[]{:S(2)}) async-start(), calls=%async_computation | async-start | bytes 524288 | tf_op jit(solution)/shard_map/psum | solution.py:23
  38.8 274.6 %all-gather.3.cloned.1.call-start = ((), (), s32[]{:S(2)}) async-start(), calls=%async_computation.1 | async-start | bytes 50823168 | tf_op jit(solution)/shard_map/all_gather | solution.py:26
Sparse Core Ops, SparseCore 0:
  38.9 112.3 all-reduce.2
  154.4 158.9 all-gather.2
